TPU v7x, 256 devices: a whole 4x4x8 slice. The times are simulated.
256 devices in a mesh: dp: 32 (over y, x, core), shard: 8 (over z).
Axes of the slice: x: 4, y: 4, z: 8, core: 2. Of those that a mesh axis runs over, the one named last changes fastest.
Arguments:
- grads: bfloat16 [2, 32, 4096, 4096], P(None, 'dp', 'shard'), may hold values from -0.5 to 0.5
- basis: float32 [2, 4096, 256], P(None, 'shard'), may hold values from -0.375 to 0.375
- weight: float32 [2, 8, 32, 16, 4096], P(None, 'shard', 'dp'), may hold values from -6 to 6
- moment_m: float32 [2, 4096, 256], P(None, 'dp'), may hold values from -6 to 6
- moment_v: float32 [2, 4096, 256], P(None, 'dp'), may hold values from 0.25 to 4
Outputs:
- new_weight: float32 [2, 8, 32, 16, 4096], P(None, 'shard', 'dp')
- new_m: float32 [2, 4096, 256], P(None, 'dp')
- new_v: float32 [2, 4096, 256], P(None, 'dp')
- new_basis: float32 [2, 4096, 256], P(None, 'shard')
All inputs are finite; a program needn't handle non-finite values.
Results may differ from a plain program's by a relative error of at most 0.0036.
Values may be sent and summed in bfloat16 or wider, within the bound.
A program may use at most 64 MiB of HBM per device.

v0:
```python
import jax
import jax.numpy as jnp
from jax import lax
from jax.sharding import PartitionSpec as P

MATS = 2
NS_STEPS = 5


def adam_step(moment_m, moment_v, projected):
    next_m = 0.9 * moment_m + 0.1 * projected
    next_v = 0.999 * moment_v + 0.001 * projected * projected
    update = 2.0 * (next_m / (1.0 - 0.9**10)) / (jnp.sqrt(next_v / (1.0 - 0.999**10)) + 1e-08)
    return (next_m, next_v, update)


def ns_turn(iterate, gram):
    return 1.5 * iterate - 0.5 * jnp.dot(iterate, gram, precision=lax.Precision.HIGHEST)


def shards(grads, basis, weight, moment_m, moment_v):
    group_index = lax.axis_index("dp")
    rows_weight = weight.shape[3]
    weights_out, firsts, seconds, bases = ([], [], [], [])
    for matrix in range(MATS):
        gradient = grads[matrix, 0]
        basis_local = basis[matrix]
        basis_bf = basis_local.astype(jnp.bfloat16)
        partial_sum = lax.psum_scatter(
            lax.dot_general(
                gradient, basis_bf, (((0,), (0,)), ((), ())), preferred_element_type=jnp.float32
            ),
            "dp",
            scatter_dimension=0,
            tiled=True,
        )
        projected = lax.psum(partial_sum, "shard")
        next_m, next_v, update = adam_step(moment_m[matrix], moment_v[matrix], projected)
        full_update = lax.all_gather(update, "dp", axis=0, tiled=True)
        basis_rows = lax.dynamic_slice_in_dim(
            basis_local, group_index * rows_weight, rows_weight, 0
        )
        delta = jnp.dot(basis_rows, full_update.T, precision=lax.Precision.HIGHEST)
        weights_out.append((weight[matrix, 0, 0] - delta).reshape(weight.shape[1:]))
        projected_bf = projected.astype(jnp.bfloat16)
        refresh_part = jnp.dot(
            gradient,
            lax.all_gather(projected_bf, "dp", axis=0, tiled=True),
            preferred_element_type=jnp.float32,
        )
        refresh = lax.psum(refresh_part, "dp")
        total_sq = lax.psum(jnp.sum(refresh * refresh), "shard")
        iterate = refresh / jnp.sqrt(total_sq + 1e-06)
        first_turn = 0
        for step in range(first_turn, NS_STEPS):
            gram = lax.psum(
                jnp.dot(iterate.T, iterate, precision=lax.Precision.HIGHEST).astype(jnp.bfloat16),
                "shard",
            ).astype(jnp.float32)
            iterate = ns_turn(iterate, gram)
        bases.append(iterate)
        firsts.append(next_m)
        seconds.append(next_v)
    return (jnp.stack(weights_out), jnp.stack(firsts), jnp.stack(seconds), jnp.stack(bases))


def solution(mesh):
    placed = (
        P(None, "dp", "shard", None),
        P(None, "shard", None),
        P(None, "shard", "dp", None, None),
        P(None, "dp", None),
        P(None, "dp", None),
    )
    return jax.shard_map(
        shards,
        mesh=mesh,
        in_specs=placed,
        out_specs=(
            P(None, "shard", "dp", None, None),
            P(None, "dp", None),
            P(None, "dp", None),
            P(None, "shard", None),
        ),
        check_vma=False,
    )
```

profile of v0, /device:TPU:1, one launch (start us, length us, event | category | flops | bytes accessed | tf_op | source)
XLA Modules:
  0.0 1018.5 jit_solution(8599303258596466312)
XLA Ops:
  7.2 0.0 reduce-scatter.5.cloned.1.call-start
  7.2 5.5 fusion.4
  12.8 0.0 reduce-scatter.3.cloned.1.call-start
  12.8 1.1 copy-done
  14.0 5.5 fusion.8
  19.5 0.0 all-reduce.18.cloned.1.call-start
  19.6 85.4 %reduce-scatter.5.cloned.1.call-done = f32[128,256]{1,0:T(8,128)} async-done(((f32[4096,256]{1,0:T(8,128)}), f32[128,256]{1,0:T(8,128)}) %reduce-scatter.5.cloned.1.call-update) | async-done | bytes 131088 | tf_op jit(solution)/shard_map/reduce_scatter | solution.py:29
  104.9 93.3 %reduce-scatter.3.cloned.1.call-done = f32[128,256]{1,0:T(8,128)} async-done(((f32[4096,256]{1,0:T(8,128)}), f32[128,256]{1,0:T(8,128)}) %reduce-scatter.3.cloned.1.call-update) | async-done | bytes 131088 | tf_op jit(solution)/shard_map/reduce_scatter | solution.py:29
  198.3 0.0 all-gather.9.cloned.1.call-start
  198.3 71.4 %all-reduce.18.cloned.1.call-done = (f32[128,256]{1,0:T(8,128)}, f32[128,256]{1,0:T(8,128)}) async-done(((f32[128,256]{1,0:T(8,128)}, f32[128,256]{1,0:T(8,128)}), (f32[128,256]{1,0:T(8,128)}, f32[128,256]{1,0:T(8,128)})) %all-reduce.18.cloned.1.call-update) | async-done | bytes 262160 | tf_op jit(solution)/shard_map/psum | solution.py:37
  269.8 2.0 add_divide_fusion.1
  271.7 0.0 all-gather.11.cloned.1.call-start
  271.8 0.5 all-gather.11.cloned.1.call-update
  272.3 0.0 all-reduce.16.cloned.1.call-start
  272.4 52.9 %all-gather.9.cloned.1.call-done = bf16[4096,256]{1,0:T(8,128)(2,1)} async-done(((bf16[128,256]{1,0:T(8,128)(2,1)}), bf16[4096,256]{1,0:T(8,128)(2,1)}) %all-gather.9.cloned.1.call-update) | async-done | bytes 2097168 | tf_op jit(solution)/shard_map/all_gather | solution.py:48
  325.3 4.9 fusion.14
  330.2 46.1 %all-gather.11.cloned.1.call-done = bf16[4096,256]{1,0:T(8,128)(2,1)} async-done(((bf16[128,256]{1,0:T(8,128)(2,1)}), bf16[4096,256]{1,0:T(8,128)(2,1)}) %all-gather.11.cloned.1.call-update) | async-done | bytes 2097168 | tf_op jit(solution)/shard_map/all_gather | solution.py:48
  376.3 4.9 fusion.17
  381.2 0.0 all-reduce.28.cloned.1.call-start
  381.3 114.6 %all-reduce.16.cloned.1.call-done = (f32[512,256]{0,1:T(8,128)}, f32[512,256]{0,1:T(8,128)}) async-done(((f32[512,256]{0,1:T(8,128)}, f32[512,256]{0,1:T(8,128)}), (f32[512,256]{0,1:T(8,128)}, f32[512,256]{0,1:T(8,128)})) %all-reduce.16.cloned.1.call-update) | async-done | bytes 1048592 | tf_op jit(solution)/shard_map/psum | solution.py:51
  495.8 2.0 multiply_reduce_fusion
  497.8 14.3 %all-reduce.1 = (f32[]{:T(128)}, f32[]{:T(128)}) all-reduce(f32[]{:T(128)} %get-tuple-element.36, f32[]{:T(128)} %get-tuple-element.37), channel_id=1, replica_groups=mesh['dp'=32,'shard'=8] {'shard'}, use_global_device_ids=true, to_apply=%region_14.0 | all-reduce | flops 2 | bytes 16 | tf_op jit(solution)/shard_map/psum | solution.py:52
  513.5 2.5 convolution_convert_fusion.4
  516.1 2.5 convolution_convert_fusion.9
  518.6 0.0 all-reduce.26.cloned.1.call-start
  518.6 68.6 %all-reduce.28.cloned.1.call-done = (bf16[256,256]{1,0:T(8,128)(2,1)}, bf16[256,256]{1,0:T(8,128)(2,1)}) async-done(((bf16[256,256]{1,0:T(8,128)(2,1)}, bf16[256,256]{1,0:T(8,128)(2,1)}), (bf16[256,256]{1,0:T(8,128)(2,1)}, bf16[256,256]{1,0:T(8,128)(2,1)})) %all-reduce.28.cloned.1.call-update) | async-done | bytes 262160 | tf_op jit(solution)/shard_map/psum | solution.py:56
  587.2 1.4 fusion.31
  588.6 1.4 fusion.25
  590.0 1.3 convolution_convert_fusion.3
  591.3 1.3 convolution_convert_fusion.8
  592.6 0.2 all-reduce.24.cloned.1.call-start
  592.8 71.3 %all-reduce.26.cloned.1.call-done = (bf16[256,256]{1,0:T(8,128)(2,1)}, bf16[256,256]{1,0:T(8,128)(2,1)}) async-done(((bf16[256,256]{1,0:T(8,128)(2,1)}, bf16[256,256]{1,0:T(8,128)(2,1)}), (bf16[256,256]{1,0:T(8,128)(2,1)}, bf16[256,256]{1,0:T(8,128)(2,1)})) %all-reduce.26.cloned.1.call-update) | async-done | bytes 262160 | tf_op jit(solution)/shard_map/psum | solution.py:56
  664.2 1.4 fusion.24
  665.6 1.4 fusion.30
  667.0 1.3 convolution_convert_fusion.7
  668.2 1.3 convolution_convert_fusion.2
  669.5 0.0 all-reduce.22.cloned.1.call-start
  669.6 71.5 %all-reduce.24.cloned.1.call-done = (bf16[256,256]{1,0:T(8,128)(2,1)}, bf16[256,256]{1,0:T(8,128)(2,1)}) async-done(((bf16[256,256]{1,0:T(8,128)(2,1)}, bf16[256,256]{1,0:T(8,128)(2,1)}), (bf16[256,256]{1,0:T(8,128)(2,1)}, bf16[256,256]{1,0:T(8,128)(2,1)})) %all-reduce.24.cloned.1.call-update) | async-done | bytes 262160 | tf_op jit(solution)/shard_map/psum | solution.py:56
  741.1 1.4 fusion.23
  742.5 1.4 fusion.29
  743.9 1.3 convolution_convert_fusion.6
  745.1 1.3 convolution_convert_fusion.1
  746.4 0.0 all-reduce.20.cloned.1.call-start
  746.5 71.5 %all-reduce.22.cloned.1.call-done = (bf16[256,256]{1,0:T(8,128)(2,1)}, bf16[256,256]{1,0:T(8,128)(2,1)}) async-done(((bf16[256,256]{1,0:T(8,128)(2,1)}, bf16[256,256]{1,0:T(8,128)(2,1)}), (bf16[256,256]{1,0:T(8,128)(2,1)}, bf16[256,256]{1,0:T(8,128)(2,1)})) %all-reduce.22.cloned.1.call-update) | async-done | bytes 262160 | tf_op jit(solution)/shard_map/psum | solution.py:56
  818.0 1.4 fusion.22
  819.4 1.4 fusion.28
  820.8 1.3 convolution_convert_fusion.5
  822.0 1.3 convolution_convert_fusion
  823.3 0.0 all-gather.5.cloned.1.call-start
  823.4 0.5 all-gather.5.cloned.1.call-update
  823.9 0.3 all-gather.7.cloned.1.call-start
  824.2 0.5 all-gather.7.cloned.1.call-update
  824.7 1.3 fusion.50
  826.0 0.8 pad_maximum_fusion.2
  826.8 68.2 %all-reduce.20.cloned.1.call-done = (bf16[256,256]{1,0:T(8,128)(2,1)}, bf16[256,256]{1,0:T(8,128)(2,1)}) async-done(((bf16[256,256]{1,0:T(8,128)(2,1)}, bf16[256,256]{1,0:T(8,128)(2,1)}), (bf16[256,256]{1,0:T(8,128)(2,1)}, bf16[256,256]{1,0:T(8,128)(2,1)})) %all-reduce.20.cloned.1.call-update) | async-done | bytes 262160 | tf_op jit(solution)/shard_map/psum | solution.py:56
  895.0 1.4 fusion.21
  896.4 1.4 fusion.27
  897.8 0.1 pad_maximum_fusion
  897.8 1.3 copy.19
  899.2 53.3 %all-gather.5.cloned.1.call-done = f32[4096,256]{1,0:T(8,128)} async-done(((f32[128,256]{1,0:T(8,128)}), f32[4096,256]{1,0:T(8,128)}) %all-gather.5.cloned.1.call-update) | async-done | bytes 4194320 | tf_op jit(solution)/shard_map/all_gather | solution.py:39
  952.4 5.7 fusion.1
  958.1 47.4 %all-gather.7.cloned.1.call-done = f32[4096,256]{1,0:T(8,128)} async-done(((f32[128,256]{1,0:T(8,128)}), f32[4096,256]{1,0:T(8,128)}) %all-gather.7.cloned.1.call-update) | async-done | bytes 4194320 | tf_op jit(solution)/shard_map/all_gather | solution.py:39
  1005.5 5.7 fusion
  1011.1 0.8 pad_maximum_fusion.1
  (21 shorter events, 0.2 us)
Async XLA Ops:
  7.2 97.8 %reduce-scatter.5.cloned.1.call-start = ((), (), s32[]{:S(2)}) async-start(), calls=%async_computation.4 | async-start | bytes 4325376 | tf_op jit(solution)/shard_map/reduce_scatter | solution.py:29
  12.8 1.2 copy-start
  12.8 185.5 %reduce-scatter.3.cloned.1.call-start = ((), (), s32[]{:S(2)}) async-start(), calls=%async_computation.2 | async-start | bytes 4325376 | tf_op jit(solution)/shard_map/reduce_scatter | solution.py:29
  19.5 250.3 %copy-start.4 = (f32[2,128,256]{2,1,0:T(8,128)S(1)}, f32[2,128,256]{2,1,0:T(8,128)}, u32[]{:S(2)}) copy-start(f32[2,128,256]{2,1,0:T(8,128)} %param.8) | copy-start | bytes 786436
  19.5 250.3 %copy-start.5 = (f32[2,128,256]{2,1,0:T(8,128)S(1)}, f32[2,128,256]{2,1,0:T(8,128)}, u32[]{:S(2)}) copy-start(f32[2,128,256]{2,1,0:T(8,128)} %param.9) | copy-start | bytes 786436
  19.5 250.2 %all-reduce.18.cloned.1.call-start = ((), (), s32[]{:S(2)}) async-start(), calls=%async_computation.9 | async-start | bytes 524288 | tf_op jit(solution)/shard_map/psum | solution.py:37
  198.3 127.0 %all-gather.9.cloned.1.call-start = ((), (), s32[]{:S(2)}) async-start(), calls=%async_computation.6 | async-start | bytes 2162688 | tf_op jit(solution)/shard_map/all_gather | solution.py:48
  271.7 104.5 %all-gather.11.cloned.1.call-start = ((), (), s32[]{:S(2)}) async-start(), calls=%async_computation.7 | async-start | bytes 2162688 | tf_op jit(solution)/shard_map/all_gather | solution.py:48
  272.3 223.5 %all-reduce.16.cloned.1.call-start = ((), (), s32[]{:S(2)}) async-start(), calls=%async_computation.8 | async-start | bytes 2097152 | tf_op jit(solution)/shard_map/psum | solution.py:51
  381.2 206.0 %all-reduce.28.cloned.1.call-start = ((), (), s32[]{:S(2)}) async-start(), calls=%async_computation.14 | async-start | bytes 524288 | tf_op jit(solution)/shard_map/psum | solution.py:56
  495.8 91.4 %copy-start.3 = (f32[512,256]{0,1:T(8,128)S(1)}, f32[512,256]{0,1:T(8,128)}, u32[]{:S(2)}) copy-start(f32[512,256]{0,1:T(8,128)} %get-tuple-element.9) | copy-start | bytes 1572868
  497.8 90.8 %copy-start.2 = (f32[512,256]{0,1:T(8,128)S(1)}, f32[512,256]{0,1:T(8,128)}, u32[]{:S(2)}) copy-start(f32[512,256]{0,1:T(8,128)} %get-tuple-element.8) | copy-start | bytes 1572868
  518.6 145.6 %all-reduce.26.cloned.1.call-start = ((), (), s32[]{:S(2)}) async-start(), calls=%async_computation.13 | async-start | bytes 524288 | tf_op jit(solution)/shard_map/psum | solution.py:56
  592.6 148.5 %all-reduce.24.cloned.1.call-start = ((), (), s32[]{:S(2)}) async-start(), calls=%async_computation.12 | async-start | bytes 524288 | tf_op jit(solution)/shard_map/psum | solution.py:56
  669.5 148.5 %all-reduce.22.cloned.1.call-start = ((), (), s32[]{:S(2)}) async-start(), calls=%async_computation.11 | async-start | bytes 524288 | tf_op jit(solution)/shard_map/psum | solution.py:56
  746.4 148.5 %all-reduce.20.cloned.1.call-start = ((), (), s32[]{:S(2)}) async-start(), calls=%async_computation.10 | async-start | bytes 524288 | tf_op jit(solution)/shard_map/psum | solution.py:56
  823.3 129.1 %all-gather.5.cloned.1.call-start = ((), (), s32[]{:S(2)}) async-start(), calls=%async_computation.3 | async-start | bytes 4325376 | tf_op jit(solution)/shard_map/all_gather | solution.py:39
  823.9 181.6 %all-gather.7.cloned.1.call-start = ((), (), s32[]{:S(2)}) async-start(), calls=%async_computation.5 | async-start | bytes 4325376 | tf_op jit(solution)/shard_map/all_gather | solution.py:39
  825.9 126.5 %copy-start.1 = (f32[2,1,1,16,4096]{4,3,2,1,0:T(8,128)S(1)}, f32[2,1,1,16,4096]{4,3,2,1,0:T(8,128)}, u32[]{:S(2)}) copy-start(f32[2,1,1,16,4096]{4,3,2,1,0:T(8,128)} %param.7) | copy-start | bytes 1572868
Sparse Core Ops, SparseCore 0:
  12.9 91.9 reduce-scatter.4
  108.9 89.3 reduce-scatter.2
  200.6 69.0 all-reduce.17
  272.7 52.5 all-gather.8
  328.3 47.9 all-gather.10
  381.3 114.4 all-reduce.15
  518.7 68.4 all-reduce.27
  592.7 71.3 all-reduce.25
  669.6 71.3 all-reduce.23
  746.5 71.3 all-reduce.21
  823.5 71.4 all-reduce.19
  897.4 54.9 all-gather.4
  955.0 50.4 all-gather.6
where the time goes:
time: 1020 us
  waiting for transfers between devices  917 us (90%)
  matrix products  61.3 us (6%)
  between operations  15.4 us (2%)
  blocking collectives  14.3 us (1%)
    psum x5, waiting for transfers between devices, shards(): lax.psum(jnp.dot(iterate.T, iterate, precision=lax.Precision.HIGHEST).ast...  351 us
    reduce_scatter x2, waiting for transfers between devices, shards(): lax.psum_scatter(lax.dot_general(gradient, basis_bf, (((0,), (0,)), ((),...  179 us
    psum x1, waiting for transfers between devices, shards(): refresh = lax.psum(refresh_part, 'dp')  115 us
    all_gather x2, waiting for transfers between devices, shards(): full_update = lax.all_gather(update, 'dp', axis=0, tiled=True)  101 us
    all_gather x2, waiting for transfers between devices, shards(): lax.all_gather(projected_bf, 'dp', axis=0, tiled=True)  99 us
    psum x1, waiting for transfers between devices, shards(): projected = lax.psum(partial_sum, 'shard')  71.4 us
  transfers between devices with their start and end apart: 13, of which 13 were waited for; matrix products, arithmetic and copies ran while one was open for 2% of the time, Pallas kernels for 0%

commit v1 on v0

--- a/solution.py
+++ b/solution.py
@@ -5,6 +5,18 @@
 
 MATS = 2
 NS_STEPS = 5
+
+
+def figure_pair(shard_in, named_axis="dp"):
+    return jnp.concatenate(
+        jax.lax.all_to_all(
+            jnp.stack([shard_in for _ in range(jax.lax.axis_size(named_axis))], axis=0),
+            named_axis,
+            0,
+            0,
+        ),
+        axis=0,
+    )
 
 
 def adam_step(moment_m, moment_v, projected):
@@ -44,9 +56,7 @@
         weights_out.append((weight[matrix, 0, 0] - delta).reshape(weight.shape[1:]))
         projected_bf = projected.astype(jnp.bfloat16)
         refresh_part = jnp.dot(
-            gradient,
-            lax.all_gather(projected_bf, "dp", axis=0, tiled=True),
-            preferred_element_type=jnp.float32,
+            gradient, figure_pair(projected_bf), preferred_element_type=jnp.float32
         )
         refresh = lax.psum(refresh_part, "dp")
         total_sq = lax.psum(jnp.sum(refresh * refresh), "shard")

time: 1020 us -> 986 us (0.967)
  waiting for transfers between devices: 917 us -> 838 us
  blocking collectives: 14.3 us -> 55.2 us
    all_gather x2 -> x0, waiting for transfers between devices: 99 us -> none  [shards(): lax.all_gather(projected_bf, 'dp', axis=0, tiled=True)]
    all_to_all x0 -> x1, blocking collectives: none -> 40.9 us  [figure_pair(): jax.lax.all_to_all(jnp.stack([shard_in for _ in range(jax.lax.axis_size(n...]
    all_to_all x0 -> x1, waiting for transfers between devices: none -> 23.3 us  [figure_pair(): jax.lax.all_to_all(jnp.stack([shard_in for _ in range(jax.lax.axis_size(n...]
  transfers between devices with their start and end apart: 13 -> 12, of which waited for: 13 -> 12; matrix products, arithmetic and copies ran while one was open for 2% -> 2% of each run, Pallas kernels for 0% -> 0%
where the time goes in v1:
time: 986 us; the launch traced here: 985 us
  waiting for transfers between devices  838 us (85%)
  matrix products  60.6 us (6%)
  blocking collectives  55.2 us (6%)
  between operations  15.4 us (2%)
    psum x5, waiting for transfers between devices, shards(): lax.psum(jnp.dot(iterate.T, iterate, precision=lax.Precision.HIGHEST).ast...  351 us
    reduce_scatter x2, waiting for transfers between devices, shards(): lax.psum_scatter(lax.dot_general(gradient, basis_bf, (((0,), (0,)), ((),...  179 us
    psum x1, waiting for transfers between devices, shards(): refresh = lax.psum(refresh_part, 'dp')  111 us
    all_gather x2, waiting for transfers between devices, shards(): full_update = lax.all_gather(update, 'dp', axis=0, tiled=True)  101 us
    psum x1, waiting for transfers between devices, shards(): projected = lax.psum(partial_sum, 'shard')  71.5 us
    all_to_all x1, blocking collectives, figure_pair(): jax.lax.all_to_all(jnp.stack([shard_in for _ in range(jax.lax.axis_size(n...  40.9 us
    all_to_all x1, waiting for transfers between devices, figure_pair(): jax.lax.all_to_all(jnp.stack([shard_in for _ in range(jax.lax.axis_size(n...  23.3 us
  transfers between devices with their start and end apart: 12, of which 12 were waited for; matrix products, arithmetic and copies ran while one was open for 2% of the time, Pallas kernels for 0%

profile of v1, /device:TPU:1, one launch (start us, length us, event | category | flops | bytes accessed | tf_op | source)
XLA Modules:
  0.0 985.4 jit_solution(14126825464938857118)
XLA Ops:
  7.2 0.0 reduce-scatter.5.cloned.1.call-start
  7.2 5.5 fusion.4
  12.8 0.0 reduce-scatter.3.cloned.1.call-start
  12.8 1.1 copy-done
  14.0 5.5 fusion.8
  19.5 0.0 all-reduce.18.cloned.1.call-start
  19.5 85.4 %reduce-scatter.5.cloned.1.call-done = f32[128,256]{1,0:T(8,128)} async-done(((f32[4096,256]{1,0:T(8,128)}), f32[128,256]{1,0:T(8,128)}) %reduce-scatter.5.cloned.1.call-update) | async-done | bytes 131088 | tf_op jit(solution)/shard_map/reduce_scatter | solution.py:41
  104.9 93.3 %reduce-scatter.3.cloned.1.call-done = f32[128,256]{1,0:T(8,128)} async-done(((f32[4096,256]{1,0:T(8,128)}), f32[128,256]{1,0:T(8,128)}) %reduce-scatter.3.cloned.1.call-update) | async-done | bytes 131088 | tf_op jit(solution)/shard_map/reduce_scatter | solution.py:41
  198.3 71.5 %all-reduce.18.cloned.1.call-done = (f32[128,256]{1,0:T(8,128)}, f32[128,256]{1,0:T(8,128)}) async-done(((f32[128,256]{1,0:T(8,128)}, f32[128,256]{1,0:T(8,128)}), (f32[128,256]{1,0:T(8,128)}, f32[128,256]{1,0:T(8,128)})) %all-reduce.18.cloned.1.call-update) | async-done | bytes 262160 | tf_op jit(solution)/shard_map/psum | solution.py:49
  269.8 2.0 add_divide_fusion.1
  271.7 0.2 stack.31
  272.0 40.9 %all_to_all.10 = bf16[32,128,256]{2,1,0:T(8,128)(2,1)} all-to-all(bf16[32,128,256]{2,1,0:T(8,128)(2,1)S(1)} %stack.31), channel_id=1, replica_groups=mesh['dp'=32,'shard'=8] {'dp'}, dimensions={0} | all-to-all | bytes 4194304 | tf_op jit(solution)/shard_map/all_to_all | solution.py:12
  312.9 1.6 stack.33
  314.4 4.1 all-to-all-start.1
  318.5 0.0 all-reduce.16.cloned.1.call-start
  318.6 4.9 fusion.14
  323.5 23.3 %all-to-all-done.1 = bf16[32,128,256]{2,1,0:T(8,128)(2,1)S(1)} async-done(((bf16[32,128,256]{2,1,0:T(8,128)(2,1)}), bf16[32,128,256]{2,1,0:T(8,128)(2,1)S(1)}, u32[]{:S(2)}, u32[]{:S(2)}) %all-to-all-start.1) | async-done | bytes 2097184 | tf_op jit(solution)/shard_map/all_to_all | solution.py:12
  346.8 4.3 fusion.17
  351.1 0.0 all-reduce.28.cloned.1.call-start
  351.2 111.4 %all-reduce.16.cloned.1.call-done = (f32[512,256]{0,1:T(8,128)}, f32[512,256]{0,1:T(8,128)}) async-done(((f32[512,256]{0,1:T(8,128)}, f32[512,256]{0,1:T(8,128)}), (f32[512,256]{0,1:T(8,128)}, f32[512,256]{0,1:T(8,128)})) %all-reduce.16.cloned.1.call-update) | async-done | bytes 1048592 | tf_op jit(solution)/shard_map/psum | solution.py:61
  462.5 2.0 multiply_reduce_fusion
  464.5 14.3 %all-reduce.1 = (f32[]{:T(128)}, f32[]{:T(128)}) all-reduce(f32[]{:T(128)} %get-tuple-element.36, f32[]{:T(128)} %get-tuple-element.37), channel_id=1, replica_groups=mesh['dp'=32,'shard'=8] {'shard'}, use_global_device_ids=true, to_apply=%region_14.0 | all-reduce | flops 2 | bytes 16 | tf_op jit(solution)/shard_map/psum | solution.py:62
  480.2 2.5 convolution_convert_fusion.4
  482.8 2.5 convolution_convert_fusion.9
  485.3 0.0 all-reduce.26.cloned.1.call-start
  485.3 68.6 %all-reduce.28.cloned.1.call-done = (bf16[256,256]{1,0:T(8,128)(2,1)}, bf16[256,256]{1,0:T(8,128)(2,1)}) async-done(((bf16[256,256]{1,0:T(8,128)(2,1)}, bf16[256,256]{1,0:T(8,128)(2,1)}), (bf16[256,256]{1,0:T(8,128)(2,1)}, bf16[256,256]{1,0:T(8,128)(2,1)})) %all-reduce.28.cloned.1.call-update) | async-done | bytes 262160 | tf_op jit(solution)/shard_map/psum | solution.py:66
  553.9 1.4 fusion.31
  555.3 1.4 fusion.25
  556.7 1.3 convolution_convert_fusion.3
  558.0 1.3 convolution_convert_fusion.8
  559.3 0.2 all-reduce.24.cloned.1.call-start
  559.5 71.4 %all-reduce.26.cloned.1.call-done = (bf16[256,256]{1,0:T(8,128)(2,1)}, bf16[256,256]{1,0:T(8,128)(2,1)}) async-done(((bf16[256,256]{1,0:T(8,128)(2,1)}, bf16[256,256]{1,0:T(8,128)(2,1)}), (bf16[256,256]{1,0:T(8,128)(2,1)}, bf16[256,256]{1,0:T(8,128)(2,1)})) %all-reduce.26.cloned.1.call-update) | async-done | bytes 262160 | tf_op jit(solution)/shard_map/psum | solution.py:66
  630.9 1.4 fusion.24
  632.3 1.4 fusion.30
  633.7 1.3 convolution_convert_fusion.7
  635.0 1.3 convolution_convert_fusion.2
  636.3 0.0 all-reduce.22.cloned.1.call-start
  636.4 71.6 %all-reduce.24.cloned.1.call-done = (bf16[256,256]{1,0:T(8,128)(2,1)}, bf16[256,256]{1,0:T(8,128)(2,1)}) async-done(((bf16[256,256]{1,0:T(8,128)(2,1)}, bf16[256,256]{1,0:T(8,128)(2,1)}), (bf16[256,256]{1,0:T(8,128)(2,1)}, bf16[256,256]{1,0:T(8,128)(2,1)})) %all-reduce.24.cloned.1.call-update) | async-done | bytes 262160 | tf_op jit(solution)/shard_map/psum | solution.py:66
  707.9 1.4 fusion.23
  709.3 1.4 fusion.29
  710.7 1.3 convolution_convert_fusion.6
  712.0 1.3 convolution_convert_fusion.1
  713.3 0.0 all-reduce.20.cloned.1.call-start
  713.3 71.5 %all-reduce.22.cloned.1.call-done = (bf16[256,256]{1,0:T(8,128)(2,1)}, bf16[256,256]{1,0:T(8,128)(2,1)}) async-done(((bf16[256,256]{1,0:T(8,128)(2,1)}, bf16[256,256]{1,0:T(8,128)(2,1)}), (bf16[256,256]{1,0:T(8,128)(2,1)}, bf16[256,256]{1,0:T(8,128)(2,1)})) %all-reduce.22.cloned.1.call-update) | async-done | bytes 262160 | tf_op jit(solution)/shard_map/psum | solution.py:66
  784.9 1.4 fusion.22
  786.2 1.4 fusion.28
  787.6 1.3 convolution_convert_fusion.5
  788.9 1.3 convolution_convert_fusion
  790.2 0.0 all-gather.3.cloned.1.call-start
  790.3 0.5 all-gather.3.cloned.1.call-update
  790.8 0.3 all-gather.5.cloned.1.call-start
  791.1 0.5 all-gather.5.cloned.1.call-update
  791.5 1.3 fusion.50
  792.8 0.8 pad_maximum_fusion.2
  793.7 68.2 %all-reduce.20.cloned.1.call-done = (bf16[256,256]{1,0:T(8,128)(2,1)}, bf16[256,256]{1,0:T(8,128)(2,1)}) async-done(((bf16[256,256]{1,0:T(8,128)(2,1)}, bf16[256,256]{1,0:T(8,128)(2,1)}), (bf16[256,256]{1,0:T(8,128)(2,1)}, bf16[256,256]{1,0:T(8,128)(2,1)})) %all-reduce.20.cloned.1.call-update) | async-done | bytes 262160 | tf_op jit(solution)/shard_map/psum | solution.py:66
  861.8 1.4 fusion.21
  863.2 1.4 fusion.27
  864.6 0.1 pad_maximum_fusion
  864.7 1.3 copy.19
  866.0 53.3 %all-gather.3.cloned.1.call-done = f32[4096,256]{1,0:T(8,128)} async-done(((f32[128,256]{1,0:T(8,128)}), f32[4096,256]{1,0:T(8,128)}) %all-gather.3.cloned.1.call-update) | async-done | bytes 4194320 | tf_op jit(solution)/shard_map/all_gather | solution.py:51
  919.3 5.7 fusion.1
  924.9 47.4 %all-gather.5.cloned.1.call-done = f32[4096,256]{1,0:T(8,128)} async-done(((f32[128,256]{1,0:T(8,128)}), f32[4096,256]{1,0:T(8,128)}) %all-gather.5.cloned.1.call-update) | async-done | bytes 4194320 | tf_op jit(solution)/shard_map/all_gather | solution.py:51
  972.4 5.7 fusion
  978.0 0.8 pad_maximum_fusion.1
  (20 shorter events, 0.2 us)
Async XLA Ops:
  7.2 97.8 %reduce-scatter.5.cloned.1.call-start = ((), (), s32[]{:S(2)}) async-start(), calls=%async_computation.6 | async-start | bytes 4325376 | tf_op jit(solution)/shard_map/reduce_scatter | solution.py:41
  12.8 1.2 copy-start
  12.8 185.5 %reduce-scatter.3.cloned.1.call-start = ((), (), s32[]{:S(2)}) async-start(), calls=%async_computation.4 | async-start | bytes 4325376 | tf_op jit(solution)/shard_map/reduce_scatter | solution.py:41
  19.5 250.3 %copy-start.4 = (f32[2,128,256]{2,1,0:T(8,128)S(1)}, f32[2,128,256]{2,1,0:T(8,128)}, u32[]{:S(2)}) copy-start(f32[2,128,256]{2,1,0:T(8,128)} %param.8) | copy-start | bytes 786436
  19.5 250.3 %copy-start.5 = (f32[2,128,256]{2,1,0:T(8,128)S(1)}, f32[2,128,256]{2,1,0:T(8,128)}, u32[]{:S(2)}) copy-start(f32[2,128,256]{2,1,0:T(8,128)} %param.9) | copy-start | bytes 786436
  19.5 250.3 %all-reduce.18.cloned.1.call-start = ((), (), s32[]{:S(2)}) async-start(), calls=%async_computation.9 | async-start | bytes 524288 | tf_op jit(solution)/shard_map/psum | solution.py:49
  314.4 32.4 %all-to-all-start.1 = ((bf16[32,128,256]{2,1,0:T(8,128)(2,1)}), bf16[32,128,256]{2,1,0:T(8,128)(2,1)S(1)}, u32[]{:S(2)}, u32[]{:S(2)}) async-start(bf16[32,128,256]{2,1,0:T(8,128)(2,1)} %stack.33), calls=%async_computation.3 | async-start | bytes 4194304 | tf_op jit(solution)/shard_map/all_to_all | solution.py:12
  318.5 144.0 %all-reduce.16.cloned.1.call-start = ((), (), s32[]{:S(2)}) async-start(), calls=%async_computation.8 | async-start | bytes 2097152 | tf_op jit(solution)/shard_map/psum | solution.py:61
  351.1 202.8 %all-reduce.28.cloned.1.call-start = ((), (), s32[]{:S(2)}) async-start(), calls=%async_computation.14 | async-start | bytes 524288 | tf_op jit(solution)/shard_map/psum | solution.py:66
  462.5 91.4 %copy-start.3 = (f32[512,256]{0,1:T(8,128)S(1)}, f32[512,256]{0,1:T(8,128)}, u32[]{:S(2)}) copy-start(f32[512,256]{0,1:T(8,128)} %get-tuple-element.9) | copy-start | bytes 1572868
  464.5 90.8 %copy-start.2 = (f32[512,256]{0,1:T(8,128)S(1)}, f32[512,256]{0,1:T(8,128)}, u32[]{:S(2)}) copy-start(f32[512,256]{0,1:T(8,128)} %get-tuple-element.8) | copy-start | bytes 1572868
  485.3 145.7 %all-reduce.26.cloned.1.call-start = ((), (), s32[]{:S(2)}) async-start(), calls=%async_computation.13 | async-start | bytes 524288 | tf_op jit(solution)/shard_map/psum | solution.py:66
  559.3 148.6 %all-reduce.24.cloned.1.call-start = ((), (), s32[]{:S(2)}) async-start(), calls=%async_computation.12 | async-start | bytes 524288 | tf_op jit(solution)/shard_map/psum | solution.py:66
  636.3 148.5 %all-reduce.22.cloned.1.call-start = ((), (), s32[]{:S(2)}) async-start(), calls=%async_computation.11 | async-start | bytes 524288 | tf_op jit(solution)/shard_map/psum | solution.py:66
  713.3 148.6 %all-reduce.20.cloned.1.call-start = ((), (), s32[]{:S(2)}) async-start(), calls=%async_computation.10 | async-start | bytes 524288 | tf_op jit(solution)/shard_map/psum | solution.py:66
  790.2 129.1 %all-gather.3.cloned.1.call-start = ((), (), s32[]{:S(2)}) async-start(), calls=%async_computation.5 | async-start | bytes 4325376 | tf_op jit(solution)/shard_map/all_gather | solution.py:51
  790.8 181.6 %all-gather.5.cloned.1.call-start = ((), (), s32[]{:S(2)}) async-start(), calls=%async_computation.7 | async-start | bytes 4325376 | tf_op jit(solution)/shard_map/all_gather | solution.py:51
  792.8 126.5 %copy-start.1 = (f32[2,1,1,16,4096]{4,3,2,1,0:T(8,128)S(1)}, f32[2,1,1,16,4096]{4,3,2,1,0:T(8,128)}, u32[]{:S(2)}) copy-start(f32[2,1,1,16,4096]{4,3,2,1,0:T(8,128)} %param.7) | copy-start | bytes 1572868
Sparse Core Ops, SparseCore 0:
  12.9 91.9 reduce-scatter.4
  108.9 89.3 reduce-scatter.2
  200.6 69.0 all-reduce.17
  351.2 111.2 all-reduce.15
  485.4 68.4 all-reduce.27
  559.4 71.4 all-reduce.25
  636.4 71.4 all-reduce.23
  713.4 71.3 all-reduce.21
  790.3 71.4 all-reduce.19
  864.3 54.9 all-gather.2
  921.8 50.4 all-gather.4
